TPU v7x, 256 devices: a whole 4x4x8 slice. The times are simulated.
256 devices in a mesh: dp: 32 (over z, y), section: 2 (over core), tensor: 4 (over x).
Axes of the slice: x: 4, y: 4, z: 8, core: 2. Of those that a mesh axis runs over, the one named last changes fastest.
Arguments:
- tokens: bfloat16 [8192, 2048], P('dp'), may hold values from -6 to 6
- base_rows: int32 [128], replicated, may hold values from 1 to 6, as said below
- baseline_owner: int32 [128], replicated, may hold values from 0 to 31, as said below
- cotangent: bfloat16 [2, 16384, 2048], P('section', 'dp'), may hold values from -6 to 6
- pre_gain: float32 [2, 2048], P('section'), may hold values from 0.25 to 1.75
- input_proj: bfloat16 [2, 2048, 2048], P('section', None, 'tensor'), may hold values from -0.125 to 0.125
- gate_proj: bfloat16 [2, 2048, 2048], P('section', None, 'tensor'), may hold values from -0.125 to 0.125
- state_proj: bfloat16 [2, 2048, 256], P('section'), may hold values from -0.125 to 0.125
- step_proj: bfloat16 [2, 2048, 32], P('section', None, 'tensor'), may hold values from -0.125 to 0.125
- step_bias: float32 [2, 32], P('section', 'tensor'), may hold values from -6 to -1.5
- decay_log: float32 [2, 32], P('section', 'tensor'), may hold values from 0 to 2.5
- skip_gain: float32 [2, 32], P('section', 'tensor'), may hold values from 0.5 to 1.5
- norm_gain: float32 [2, 2048], P('section', 'tensor'), may hold values from 0.25 to 1.75
- out_proj: bfloat16 [2, 2048, 2048], P('section', 'tensor'), may hold values from -0.125 to 0.125
Outputs:
- activations: bfloat16 [2, 16384, 2048], P('section', 'dp')
- out_grad: bfloat16 [2, 2048, 2048], P('section', 'tensor', 'dp')
Inputs may be any that keep to these rules, and one draw needn't show every extreme that they name: `base_rows`: over all baselines they sum to 256; some baseline has exactly 6. `baseline_owner`: every owner holds exactly 4 baselines; the base_rows of one owner's baselines sum to at most 16, and for some owner to exactly 16.
All inputs are finite; a program needn't handle non-finite values.
Results may differ from a plain program's by a relative error of at most 0.025.
Values may be sent and summed in bfloat16 or wider, within the bound.
A program may use at most 128 MiB of HBM per device.

v0:
```python
import jax
import jax.numpy as jnp
from jax import lax
from jax.sharding import PartitionSpec as P

HEADS = 32
HEADDIM = 64
NSTATE = 128
BLOCK = 64
MICRO = 2
EPS = 1e-05


def from_behind(value, axis, steps):
    count = lax.axis_size(axis)
    first, last = (max(0, -steps), min(count, count - steps))
    return lax.ppermute(value, axis, [(source, source + steps) for source in range(first, last)])


def layout_tables(base_rows, baseline_owner):
    count = base_rows.shape[0]
    index = jnp.arange(count, dtype=jnp.int32)
    ends = jnp.cumsum(base_rows)
    starts = ends - base_rows
    earlier = (baseline_owner[:, None] == baseline_owner[None, :]) & (
        index[None, :] < index[:, None]
    )
    owner_start = jnp.sum(jnp.where(earlier, base_rows[None, :], 0), axis=1)
    return (index, starts, ends, owner_start)


def block_scan(
    heads_in, b_rows, c_rows, step_size, decay_rate, segment, state, prev_segment, block
):
    total_rows, head_count, head_dim = heads_in.shape
    blocks = total_rows // block

    def advance(carried_in, item):
        state_now, segment_before = carried_in
        x_blk, b_blk, c_blk, dt_blk, seg_blk = item
        running = jnp.cumsum(dt_blk * decay_rate[None, :], axis=0)
        positions = jnp.arange(block, dtype=jnp.int32)
        together = (seg_blk[:, None] == seg_blk[None, :]) & (
            positions[:, None] >= positions[None, :]
        )
        spread = jnp.minimum(running[:, None, :] - running[None, :, :], 0.0)
        decay_mask = jnp.where(together[:, :, None], jnp.exp(spread), 0.0)
        scores = jnp.dot(c_blk, b_blk.T, preferred_element_type=jnp.float32)
        weights = (decay_mask * scores[:, :, None] * dt_blk[None, :, :]).astype(jnp.bfloat16)
        within = jnp.einsum("ijh,jhp->ihp", weights, x_blk, preferred_element_type=jnp.float32)
        keep_in = (seg_blk == segment_before).astype(jnp.float32)
        readout = jnp.einsum(
            "in,hpn->ihp", c_blk, state_now.astype(jnp.bfloat16), preferred_element_type=jnp.float32
        )
        from_state = keep_in[:, None, None] * jnp.exp(running)[:, :, None] * readout
        last_segment = seg_blk[-1]
        tail_weight = (
            jnp.where(
                (seg_blk == last_segment)[:, None], jnp.exp(running[-1][None, :] - running), 0.0
            )
            * dt_blk
        )
        scaled = (tail_weight[:, :, None] * x_blk.astype(jnp.float32)).astype(jnp.bfloat16)
        fresh_term = jnp.einsum("jhp,jn->hpn", scaled, b_blk, preferred_element_type=jnp.float32)
        keep_state = (last_segment == segment_before).astype(jnp.float32)
        state_next = keep_state * jnp.exp(running[-1])[:, None, None] * state_now + fresh_term
        return ((state_next, last_segment), within + from_state)

    scanned = (
        heads_in.reshape(blocks, block, head_count, head_dim),
        b_rows.reshape(blocks, block, -1),
        c_rows.reshape(blocks, block, -1),
        step_size.reshape(blocks, block, head_count),
        segment.reshape(blocks, block),
    )
    (state, prev_segment), outputs = lax.scan(advance, (state, prev_segment), scanned)
    return (outputs.reshape(total_rows, head_count, head_dim), state, prev_segment)


def block_layer(rows_in, segment, carried_state, params):
    (
        pre_gain,
        input_proj,
        gate_proj,
        state_proj,
        step_proj,
        step_bias,
        decay_log,
        skip_gain,
        norm_gain,
        out_proj,
    ) = params
    row_count = rows_in.shape[0]
    local_heads = step_proj.shape[1]
    rows_f = rows_in.astype(jnp.float32)
    normed = (
        rows_f * lax.rsqrt(jnp.mean(rows_f * rows_f, axis=-1, keepdims=True) + EPS) * pre_gain
    ).astype(jnp.bfloat16)
    scan_in = jax.nn.silu(jnp.dot(normed, input_proj, preferred_element_type=jnp.float32)).astype(
        jnp.bfloat16
    )
    gate_pre = jnp.dot(normed, gate_proj, preferred_element_type=jnp.float32)
    state_io = jax.nn.silu(jnp.dot(normed, state_proj, preferred_element_type=jnp.float32)).astype(
        jnp.bfloat16
    )
    step_size = jax.nn.softplus(
        jnp.dot(normed, step_proj, preferred_element_type=jnp.float32) + step_bias
    )
    decay_rate = -jnp.exp(decay_log)
    heads_in = scan_in.reshape(row_count, local_heads, HEADDIM)
    scan_out, state_end, segment_end = block_scan(
        heads_in,
        state_io[:, :NSTATE],
        state_io[:, NSTATE:],
        step_size,
        decay_rate,
        segment,
        carried_state[0],
        carried_state[1],
        BLOCK,
    )
    scan_out = scan_out + skip_gain[None, :, None] * heads_in.astype(jnp.float32)
    gated = scan_out.reshape(row_count, local_heads * HEADDIM) * jax.nn.silu(gate_pre)
    sq_sum = lax.psum(jnp.sum(gated * gated, axis=-1), "tensor")
    y_norm = (gated * lax.rsqrt(sq_sum[:, None] / (HEADS * HEADDIM) + EPS) * norm_gain).astype(
        jnp.bfloat16
    )
    row_share = row_count // lax.axis_size("tensor")
    summed = lax.psum_scatter(
        jnp.dot(y_norm, out_proj, preferred_element_type=jnp.float32).astype(jnp.bfloat16),
        "tensor",
        scatter_dimension=0,
        tiled=True,
    ).astype(jnp.float32)
    own_rows = lax.dynamic_slice_in_dim(rows_f, lax.axis_index("tensor") * row_share, row_share, 0)
    own_out = (own_rows + summed).astype(jnp.bfloat16)
    result = lax.all_gather(own_out, "tensor", axis=0, tiled=True)
    return (result, y_norm, (state_end, segment_end))


def grad_term(y_norm, cot_rows):
    return lax.dot_general(
        y_norm, cot_rows, (((0,), (0,)), ((), ())), preferred_element_type=jnp.float32
    )


def per_device(
    tokens,
    base_rows,
    baseline_owner,
    cotangent,
    pre_gain,
    input_proj,
    gate_proj,
    state_proj,
    step_proj,
    step_bias,
    decay_log,
    skip_gain,
    norm_gain,
    out_proj,
):
    dp_count = lax.axis_size("dp")
    tok_rows, feat_width = tokens.shape
    slot_cap = 2 * tok_rows // dp_count
    own_slots = slot_cap * dp_count
    index, starts, ends, owner_start = layout_tables(base_rows, baseline_owner)
    local = jnp.arange(tok_rows, dtype=jnp.int32)
    inside = ((starts[None, :] <= local[:, None]) & (local[:, None] < ends[None, :])).astype(
        jnp.int32
    )
    row_start = jnp.sum(inside * starts[None, :], axis=1)
    row_owner = jnp.sum(inside * baseline_owner[None, :], axis=1)
    row_ostart = jnp.sum(inside * owner_start[None, :], axis=1)
    send_slot = row_owner * slot_cap + row_ostart + local - row_start
    outgoing = (
        jnp.zeros((own_slots, feat_width), jnp.bfloat16)
        .at[send_slot]
        .set(tokens)
        .reshape(dp_count, slot_cap, feat_width)
    )
    owner_index = lax.axis_index("dp")
    place = jnp.arange(slot_cap, dtype=jnp.int32)
    held = (
        (baseline_owner[None, :] == owner_index)
        & (owner_start[None, :] <= place[:, None])
        & (place[:, None] < owner_start[None, :] + base_rows[None, :])
    ).astype(jnp.int32)
    got_start = jnp.sum(held * owner_start[None, :], axis=1)
    got_len = jnp.sum(held * base_rows[None, :], axis=1)
    got_id = jnp.sum(held * index[None, :], axis=1)
    got_any = jnp.sum(held, axis=1)
    sender = jnp.arange(dp_count, dtype=jnp.int32)[:, None]
    recv_slot = (
        dp_count * got_start[None, :]
        + sender * got_len[None, :]
        + place[None, :]
        - got_start[None, :]
    )
    recv_slot = jnp.where(got_any[None, :] > 0, recv_slot, own_slots).reshape(-1)
    id_rows = jnp.broadcast_to(got_id[None, :], (dp_count, slot_cap)).reshape(-1)
    slot_ids = jnp.full((own_slots,), -1, jnp.int32).at[recv_slot].set(id_rows, mode="drop")
    arrived = lax.all_to_all(outgoing, "dp", split_axis=0, concat_axis=0, tiled=True)
    width = arrived.shape[-1]
    stream = (
        jnp.zeros((own_slots, width), jnp.bfloat16)
        .at[recv_slot]
        .set(arrived.reshape(-1, width), mode="drop")
    )
    starts_flag = jnp.concatenate(
        [jnp.ones((1,), jnp.int32), (slot_ids[1:] != slot_ids[:-1]).astype(jnp.int32)]
    )
    segment = jnp.cumsum(starts_flag)
    section_idx = lax.axis_index("section")
    params = (
        pre_gain[0],
        input_proj[0],
        gate_proj[0],
        state_proj[0],
        step_proj[0],
        step_bias[0],
        decay_log[0],
        skip_gain[0],
        norm_gain[0],
        out_proj[0],
    )
    local_heads = step_proj.shape[2]
    micro_rows = own_slots // MICRO
    zero_state = (jnp.zeros((local_heads, HEADDIM, NSTATE), jnp.float32), jnp.array(-1, jnp.int32))
    cot_own = cotangent[0]
    carried_state = zero_state
    handed = jnp.zeros((micro_rows, feat_width), jnp.bfloat16)
    outputs_all = jnp.zeros((own_slots, feat_width), jnp.bfloat16)
    grad_acc = jnp.zeros((out_proj.shape[1], feat_width), jnp.float32)
    for turn_index in range(MICRO + 1):
        micro_index = turn_index - section_idx
        active_turn = (micro_index >= 0) & (micro_index < MICRO)
        micro_index = jnp.clip(micro_index, 0, MICRO - 1)
        first_row = micro_index * micro_rows
        own_in = lax.dynamic_slice_in_dim(stream, first_row, micro_rows, 0)
        source = jnp.where(section_idx == 0, own_in, handed)
        seg_part = lax.dynamic_slice_in_dim(segment, first_row, micro_rows, 0)
        result, y_norm, moved = block_layer(source, seg_part, carried_state, params)
        carried_state = jax.tree.map(
            lambda new_val, old_val: jnp.where(active_turn, new_val, old_val), moved, carried_state
        )
        outputs_all = jnp.where(
            active_turn,
            lax.dynamic_update_slice_in_dim(outputs_all, result, first_row, 0),
            outputs_all,
        )
        cot_part = lax.dynamic_slice_in_dim(cot_own, first_row, micro_rows, 0)
        grad_acc = grad_acc + jnp.where(active_turn, grad_term(y_norm, cot_part), 0.0)
        if turn_index < MICRO:
            handed = from_behind(result, "section", 1)
    grad_share = lax.psum_scatter(
        grad_acc.astype(jnp.bfloat16), "dp", scatter_dimension=1, tiled=True
    )
    return (outputs_all[None], grad_share[None])


def solution(mesh):
    return jax.shard_map(
        per_device,
        mesh=mesh,
        in_specs=(
            P("dp", None),
            P(),
            P(),
            P("section", "dp", None),
            P("section", None),
            P("section", None, "tensor"),
            P("section", None, "tensor"),
            P("section", None, None),
            P("section", None, "tensor"),
            P("section", "tensor"),
            P("section", "tensor"),
            P("section", "tensor"),
            P("section", "tensor"),
            P("section", "tensor", None),
        ),
        out_specs=(P("section", "dp", None), P("section", "tensor", "dp")),
        check_vma=False,
    )
```

profile of v0, /device:TPU:2, one launch (start us, length us, event | category | flops | bytes accessed | tf_op | source)
XLA Modules:
  0.0 645.6 jit_solution(3707332609720669846)
XLA Ops:
  7.2 1.0 select_reduce_fusion.3
  10.8 4.4 scatter_custom_fusion
  15.2 11.8 %all-to-all-start = ((bf16[32,16,2048]{2,1,0:T(8,128)(2,1)}), bf16[32,16,2048]{2,1,0:T(8,128)(2,1)}, u32[]{:S(2)}, u32[]{:S(2)}) async-start(bf16[32,16,2048]{2,1,0:T(8,128)(2,1)} %bitcast.297), calls=%async_computation | async-start | bytes 4194304 | tf_op jit(solution)/shard_map/all_to_all | solution.py:203
  28.2 2.4 scatter_custom_fusion.2
  32.2 44.9 %all-to-all-done = bf16[32,16,2048]{2,1,0:T(8,128)(2,1)} async-done(((bf16[32,16,2048]{2,1,0:T(8,128)(2,1)}), bf16[32,16,2048]{2,1,0:T(8,128)(2,1)}, u32[]{:S(2)}, u32[]{:S(2)}) %all-to-all-start) | async-done | bytes 2097184 | tf_op jit(solution)/shard_map/all_to_all | solution.py:203
  77.1 6.1 scatter_custom_fusion.1
  83.2 1.6 multiply_reduce_fusion.2
  84.9 1.7 compare_select_fusion.2
  87.4 2.2 multiply_convert_fusion.20
  91.4 1.1 broadcast.415.clone2
  92.4 33.7 %while.45 = (s32[]{:T(128)}, f32[8,64,128]{2,1,0:T(8,128)S(1)}, s32[]{:T(128)}, f32[4,64,8,64]{3,2,1,0:T(8,128)}, s32[4,64]{1,0:T(4,128)S(1)}, /*index=5*/f32[4,...) while((s32[]{:T(128)}, f32[8,64,128]{2,1,0:T(8,128)S(1)}, ...), condition=%wide.region_17.18_spmd.clone, body=%wide.region_15.17_spmd.clone.sunk | while | flops 22689996 | bytes 2389582 | solution.py:76
  98.6 0.9 convolution_add_fusion.11
  107.0 0.9 convolution_add_fusion.11
  115.4 0.9 convolution_add_fusion.11
  126.2 1.5 reshape.687
  127.7 2.9 multiply_reduce_fusion.5
  130.6 8.6 %psum.21 = f32[256]{0:T(256)S(1)} all-reduce(f32[256]{0:T(256)S(1)} %get-tuple-element.392), channel_id=1, replica_groups=mesh['dp'=32,'section'=2,'tensor'=4] {'tensor'}, use_global_device_ids=true, to_apply=%region_19.20 | all-reduce | flops 256 | bytes 2048 | tf_op jit(solution)/shard_map/psum | solution.py:124
  139.2 3.4 convolution_convert_fusion.2
  142.7 2.8 fusion.116
  145.5 18.4 %reduce-scatter.5.cloned.1.call-done = bf16[64,2048]{1,0:T(8,128)(2,1)} async-done(((bf16[256,2048]{1,0:T(8,128)(2,1)}), bf16[64,2048]{1,0:T(8,128)(2,1)}) %reduce-scatter.5.cloned.1.call-update) | async-done | bytes 262160 | tf_op jit(solution)/shard_map/reduce_scatter | solution.py:129
  163.9 1.9 add_convert_fusion.3
  165.9 27.4 %all-gather.4.cloned.1.call-done = bf16[256,2048]{1,0:T(8,128)(2,1)} async-done(((bf16[64,2048]{1,0:T(8,128)(2,1)}), bf16[256,2048]{1,0:T(8,128)(2,1)}) %all-gather.4.cloned.1.call-update) | async-done | bytes 1048592 | tf_op jit(solution)/shard_map/all_gather | solution.py:137
  193.3 2.3 collective-permute-start
  196.3 0.9 collective-permute-done
  197.2 3.0 fusion.154
  202.4 1.0 copy-done.28
  204.4 1.1 reshape_reshape.10
  205.5 1.0 broadcast.415.clone2.1
  206.5 30.9 %while.43 = (s32[]{:T(128)}, f32[8,64,128]{2,1,0:T(8,128)S(1)}, s32[]{:T(128)}, f32[4,64,8,64]{3,2,1,0:T(8,128)}, s32[4,64]{1,0:T(4,128)}, /*index=5*/f32[4,64,8...) while((s32[]{:T(128)}, f32[8,64,128]{2,1,0:T(8,128)S(1)}, ...), condition=%wide.region_24.25_spmd, body=%wide.region_22.24_spmd.sunk | while | flops 22624460 | bytes 2581539 | solution.py:76
  210.3 0.9 constant_dynamic-slice_fusion.12
  218.0 0.9 constant_dynamic-slice_fusion.12
  225.8 0.9 constant_dynamic-slice_fusion.12
  233.5 0.9 constant_dynamic-slice_fusion.12
  237.4 2.3 reshape.692
  239.7 3.0 multiply_reduce_fusion.4
  242.8 9.2 %psum.22 = f32[256]{0:T(256)S(1)} all-reduce(f32[256]{0:T(256)S(1)} %get-tuple-element.394), channel_id=1, replica_groups=mesh['dp'=32,'section'=2,'tensor'=4] {'tensor'}, use_global_device_ids=true, to_apply=%region_26.27 | all-reduce | flops 256 | bytes 2048 | tf_op jit(solution)/shard_map/psum | solution.py:124
  252.0 3.3 convolution_convert_fusion.1
  255.4 24.6 %reduce-scatter.7.cloned.1.call-done = bf16[64,2048]{1,0:T(8,128)(2,1)} async-done(((bf16[256,2048]{1,0:T(8,128)(2,1)}), bf16[64,2048]{1,0:T(8,128)(2,1)}) %reduce-scatter.7.cloned.1.call-update) | async-done | bytes 262160 | tf_op jit(solution)/shard_map/reduce_scatter | solution.py:129
  280.0 1.9 add_convert_fusion.2
  282.0 27.4 %all-gather.6.cloned.1.call-done = bf16[256,2048]{1,0:T(8,128)(2,1)} async-done(((bf16[64,2048]{1,0:T(8,128)(2,1)}), bf16[256,2048]{1,0:T(8,128)(2,1)}) %all-gather.6.cloned.1.call-update) | async-done | bytes 1048592 | tf_op jit(solution)/shard_map/all_gather | solution.py:137
  309.4 2.3 collective-permute-start.1
  311.8 1.5 collective-permute-done.1
  313.3 3.0 fusion.153
  318.5 1.0 copy-done.29
  320.5 1.1 reshape_reshape.11
  321.6 1.0 broadcast.415.clone
  322.6 22.8 %while.44 = (s32[]{:T(128)}, f32[8,64,128]{2,1,0:T(8,128)S(1)}, s32[]{:T(128)}, f32[4,64,8,64]{3,2,1,0:T(8,128)}, s32[4,64]{1,0:T(4,128)S(1)}, /*index=5*/f32[4,...) while((s32[]{:T(128)}, f32[8,64,128]{2,1,0:T(8,128)S(1)}, ...), condition=%wide.region_31.32_spmd, body=%wide.region_29.31_spmd.sunk | while | flops 22624460 | bytes 2582019 | solution.py:76
  325.1 0.9 constant_dynamic-slice_fusion.13
  330.7 0.9 constant_dynamic-slice_fusion.13
  336.4 0.9 constant_dynamic-slice_fusion.13
  342.1 0.9 constant_dynamic-slice_fusion.13
  345.4 1.5 reshape.697
  346.9 2.8 multiply_reduce_fusion.3
  349.8 9.2 %psum.23 = f32[256]{0:T(256)S(1)} all-reduce(f32[256]{0:T(256)S(1)} %get-tuple-element.396), channel_id=1, replica_groups=mesh['dp'=32,'section'=2,'tensor'=4] {'tensor'}, use_global_device_ids=true, to_apply=%region_33.34 | all-reduce | flops 256 | bytes 2048 | tf_op jit(solution)/shard_map/psum | solution.py:124
  359.0 3.3 convolution_convert_fusion
  362.4 24.6 %reduce-scatter.9.cloned.1.call-done = bf16[64,2048]{1,0:T(8,128)(2,1)} async-done(((bf16[256,2048]{1,0:T(8,128)(2,1)}), bf16[64,2048]{1,0:T(8,128)(2,1)}) %reduce-scatter.9.cloned.1.call-update) | async-done | bytes 262160 | tf_op jit(solution)/shard_map/reduce_scatter | solution.py:129
  387.0 1.9 add_convert_fusion.1
  390.9 2.5 add_convert_fusion
  393.6 0.9 copy-done.10
  395.3 1.3 copy-done.1
  396.6 1.3 copy.198
  397.9 18.4 %all-gather.8.cloned.1.call-done = bf16[256,2048]{1,0:T(8,128)(2,1)} async-done(((bf16[64,2048]{1,0:T(8,128)(2,1)}), bf16[256,2048]{1,0:T(8,128)(2,1)}) %all-gather.8.cloned.1.call-update) | async-done | bytes 1048592 | tf_op jit(solution)/shard_map/all_gather | solution.py:137
  416.4 2.6 bitcast_dynamic-update-slice_fusion
  419.0 219.8 %reduce-scatter.11.cloned.1.call-done = bf16[512,64]{0,1:T(8,128)(2,1)} async-done(((bf16[512,2048]{0,1:T(8,128)(2,1)}), bf16[512,64]{0,1:T(8,128)(2,1)}) %reduce-scatter.11.cloned.1.call-update) | async-done | bytes 65552 | tf_op jit(solution)/shard_map/reduce_scatter | solution.py:256
  (407 shorter events, 79.5 us)
Async XLA Ops:
  7.2 381.8 %copy-start = (bf16[1,512,2048]{2,1,0:T(8,128)(2,1)S(1)}, bf16[1,512,2048]{2,1,0:T(8,128)(2,1)}, u32[]{:S(2)}) copy-start(bf16[1,512,2048]{2,1,0:T(8,128)(2,1)} %param.23) | copy-start | bytes 6291460
  15.2 11.9 %copy-start.26 = (f32[1,8]{1,0:T(1,128)S(1)}, f32[1,8]{1,0:T(1,128)}, u32[]{:S(2)}) copy-start(f32[1,8]{1,0:T(1,128)} %param.31) | copy-start | bytes 100
  15.2 12.6 %copy-start.20 = (s32[128]{0:T(128)S(1)}, s32[128]{0:T(128)}, u32[]{:S(2)}) copy-start(s32[128]{0:T(128)} %param.22) | copy-start | bytes 1540
  15.2 12.7 %copy-start.19 = (s32[128]{0:T(128)S(1)}, s32[128]{0:T(128)}, u32[]{:S(2)}) copy-start(s32[128]{0:T(128)} %param.21) | copy-start | bytes 1540
  15.2 17.0 %copy-start.38 = (f32[1,8]{1,0:T(1,128)S(1)}, f32[1,8]{1,0:T(1,128)}, u32[]{:S(2)}) copy-start(f32[1,8]{1,0:T(1,128)} %param.30) | copy-start | bytes 100
  15.2 61.9 %all-to-all-start = ((bf16[32,16,2048]{2,1,0:T(8,128)(2,1)}), bf16[32,16,2048]{2,1,0:T(8,128)(2,1)}, u32[]{:S(2)}, u32[]{:S(2)}) async-start(bf16[32,16,2048]{2,1,0:T(8,128)(2,1)} %bitcast.297), calls=%async_computation | async-start | bytes 4194304 | tf_op jit(solution)/shard_map/all_to_all | solution.py:203
  27.0 57.9 %copy-start.32 = (bf16[1,2048,8]{1,2,0:T(8,128)(2,1)S(1)}, bf16[1,2048,8]{1,2,0:T(8,128)(2,1)}, u32[]{:S(2)}) copy-start(bf16[1,2048,8]{1,2,0:T(8,128)(2,1)} %param.28) | copy-start | bytes 98308
  27.0 57.9 %copy-start.35 = (f32[1,2048]{1,0:T(1,128)S(1)}, f32[1,2048]{1,0:T(1,128)}, u32[]{:S(2)}) copy-start(f32[1,2048]{1,0:T(1,128)} %param.24) | copy-start | bytes 24580
  27.0 57.9 %copy-start.39 = (f32[1,8]{1,0:T(1,128)S(1)}, f32[1,8]{1,0:T(1,128)}, u32[]{:S(2)}) copy-start(f32[1,8]{1,0:T(1,128)} %param.29) | copy-start | bytes 100
  27.0 137.0 %reduce-scatter.5.cloned.1.call-start = ((), (), s32[]{:S(2)}) async-start(), calls=%async_computation.5 | async-start | bytes 1310720 | tf_op jit(solution)/shard_map/reduce_scatter | solution.py:129
  84.8 5.4 copy-start.24
  87.4 2.9 copy-start.2
  87.4 2.9 copy-start.27
  91.1 1.4 copy-start.14
  92.4 4.2 copy-start.17
  97.5 2.7 copy-start.18
  100.8 4.3 copy-start.17
  105.9 2.7 copy-start.18
  109.3 4.3 copy-start.17
  114.4 2.7 copy-start.18
  117.7 4.3 copy-start.17
  122.8 2.7 copy-start.18
  127.7 11.6 %copy-start.11 = (f32[1,512]{1,0:T(1,128)S(1)}, f32[1,512]{1,0:T(1,128)}, u32[]{:S(2)}) copy-start(f32[1,512]{1,0:T(1,128)} %param.32) | copy-start | bytes 6148
  130.5 12.0 %copy-start.5 = (f32[256,512]{1,0:T(8,128)}, f32[256,512]{1,0:T(8,128)S(1)}, u32[]{:S(2)}) copy-start(f32[256,512]{1,0:T(8,128)S(1)} %get-tuple-element.393) | copy-start | bytes 1572868
  139.2 3.4 copy-start.15
  142.6 50.7 %all-gather.4.cloned.1.call-start = ((), (), s32[]{:S(2)}) async-start(), calls=%async_computation.6 | async-start | bytes 1310720 | tf_op jit(solution)/shard_map/all_gather | solution.py:137
  142.7 52.9 %copy-start.22 = (s32[256]{0:T(256)S(1)}, s32[256]{0:T(256)}, u32[]{:S(2)}) copy-start(s32[256]{0:T(256)} %get-tuple-element.388) | copy-start | bytes 3076
  165.9 114.2 %reduce-scatter.7.cloned.1.call-start = ((), (), s32[]{:S(2)}) async-start(), calls=%async_computation.7 | async-start | bytes 1310720 | tf_op jit(solution)/shard_map/reduce_scatter | solution.py:129
  193.3 3.9 collective-permute-start
  196.3 4.3 copy-start.33
  196.3 4.3 copy-start.36
  196.3 4.3 copy-start.40
  200.2 2.2 copy-start.4
  200.2 1.6 copy-start.30
  200.5 1.8 copy-start.25
  201.8 1.6 copy-start.28
  204.2 2.3 copy-start.13
  242.8 12.6 %copy-start.7 = (f32[256,512]{1,0:T(8,128)}, f32[256,512]{1,0:T(8,128)S(1)}, u32[]{:S(2)}) copy-start(f32[256,512]{1,0:T(8,128)S(1)} %get-tuple-element.395) | copy-start | bytes 1572868
  255.3 56.3 %copy-start.21 = (s32[256]{0:T(256)S(1)}, s32[256]{0:T(256)}, u32[]{:S(2)}) copy-start(s32[256]{0:T(256)} %get-tuple-element.387) | copy-start | bytes 3076
  255.4 54.0 %all-gather.6.cloned.1.call-start = ((), (), s32[]{:S(2)}) async-start(), calls=%async_computation.8 | async-start | bytes 1310720 | tf_op jit(solution)/shard_map/all_gather | solution.py:137
  281.9 105.1 %reduce-scatter.9.cloned.1.call-start = ((), (), s32[]{:S(2)}) async-start(), calls=%async_computation.9 | async-start | bytes 1310720 | tf_op jit(solution)/shard_map/reduce_scatter | solution.py:129
  309.4 3.9 collective-permute-start.1
  311.8 4.8 copy-start.34
  311.8 4.8 copy-start.37
  311.8 4.8 copy-start.41
  316.3 2.2 copy-start.3
  316.3 1.6 copy-start.31
  317.9 1.6 copy-start.29
  320.3 2.3 copy-start.12
  322.6 24.3 %copy-start.23 = (f32[512]{0:T(512)S(1)}, f32[512]{0:T(512)}, u32[]{:S(2)}) copy-start(f32[512]{0:T(512)} %mul.547) | copy-start | bytes 6148
  362.3 26.7 %copy-start.6 = (f32[256,512]{1,0:T(8,128)S(1)}, f32[256,512]{1,0:T(8,128)}, u32[]{:S(2)}) copy-start(f32[256,512]{1,0:T(8,128)} %copy-done.5) | copy-start | bytes 1572868
  362.3 26.7 %copy-start.16 = (f32[256]{0:T(256)S(1)}, f32[256]{0:T(256)}, u32[]{:S(2)}) copy-start(f32[256]{0:T(256)} %copy-done.15) | copy-start | bytes 3076
  362.3 54.0 %all-gather.8.cloned.1.call-start = ((), (), s32[]{:S(2)}) async-start(), calls=%async_computation.10 | async-start | bytes 1310720 | tf_op jit(solution)/shard_map/all_gather | solution.py:137
  388.9 249.8 %reduce-scatter.11.cloned.1.call-start = ((), (), s32[]{:S(2)}) async-start(), calls=%async_computation.11 | async-start | bytes 2162688 | tf_op jit(solution)/shard_map/reduce_scatter | solution.py:256
  389.0 1.0 copy-start.8
  393.3 1.2 copy-start.10
  393.4 1.5 copy-start.9
  395.3 1.3 copy-start.1
Sparse Core Ops, SparseCore 0:
  142.7 21.1 reduce-scatter.4
  166.0 27.2 all-gather.3
  255.5 24.5 reduce-scatter.6
  282.0 27.2 all-gather.5
  362.5 24.5 reduce-scatter.8
  389.1 27.2 all-gather.7
  421.2 217.4 reduce-scatter.10
where the time goes:
time: 648 us; the launch traced here: 646 us
  waiting for transfers between devices  408 us (63%)
  local copies, waits for them, and re-layouts  66.8 us (10%)
  matrix products  51.8 us (8%)
  other arithmetic  44.7 us (7%)
  blocking collectives  27 us (4%)
  starting transfers between devices  16.6 us (3%)
  loops' own time  15.7 us (2%)
  between operations  14.8 us (2%)
    reduce_scatter x1, waiting for transfers between devices, per_device(): lax.psum_scatter(grad_acc.astype(jnp.bfloat16), 'dp', scatter_dimension=1...  220 us
    all_gather x3, waiting for transfers between devices, block_layer(): result = lax.all_gather(own_out, 'tensor', axis=0, tiled=True)  73.3 us
    reduce_scatter x3, waiting for transfers between devices, block_layer(): lax.psum_scatter(jnp.dot(y_norm, out_proj, preferred_element_type=jnp.flo...  67.7 us
    all_to_all x1, waiting for transfers between devices, per_device(): lax.all_to_all(outgoing, 'dp', split_axis=0, concat_axis=0, tiled=True)  44.9 us
    psum x3, blocking collectives, block_layer(): sq_sum = lax.psum(jnp.sum(gated * gated, axis=-1), 'tensor')  27 us
    another operation x3, loops' own time, block_scan(): lax.scan(advance, (state, prev_segment), scanned)  15.7 us
  transfers between devices with their start and end apart: 10, of which 10 were waited for; matrix products, arithmetic and copies ran while one was open for 3% of the time, Pallas kernels for 0%

commit v1 on v0

--- a/solution.py
+++ b/solution.py
@@ -134,7 +134,16 @@
     ).astype(jnp.float32)
     own_rows = lax.dynamic_slice_in_dim(rows_f, lax.axis_index("tensor") * row_share, row_share, 0)
     own_out = (own_rows + summed).astype(jnp.bfloat16)
-    result = lax.all_gather(own_out, "tensor", axis=0, tiled=True)
+    ways = lax.axis_size("tensor")
+    up = [(d, (d + 1) % ways) for d in range(ways)]
+    down = [(d, (d - 1) % ways) for d in range(ways)]
+    earlier_2, later = ([own_out], [own_out])
+    for _ in range(ways // 2):
+        earlier_2.append(lax.ppermute(earlier_2[-1], "tensor", up))
+    for _ in range((ways - 1) // 2):
+        later.append(lax.ppermute(later[-1], "tensor", down))
+    line = jnp.concatenate([*earlier_2[::-1], *later[1:]], axis=0)
+    result = jnp.roll(line, (lax.axis_index("tensor") - ways // 2) * own_out.shape[0], axis=0)
     return (result, y_norm, (state_end, segment_end))
 
 

time: 648 us -> 618 us (0.954); the launches traced: 646 us -> 609 us
  waiting for transfers between devices: 408 us -> 340 us
  other arithmetic: 44.7 us -> 56.7 us
  starting transfers between devices: 16.6 us -> 28.3 us
    all_gather x3 -> x0, waiting for transfers between devices: 73.3 us -> none  [block_layer(): result = lax.all_gather(own_out, 'tensor', axis=0, tiled=True)]
    ppermute x0 -> x9, waiting for transfers between devices: none -> 30.1 us  [the longest x6 30.1 us: block_layer(): earlier_2.append(lax.ppermute(earlier_2[-1], 'tensor', up))]
    reduce_scatter x1, waiting for transfers between devices: 220 us -> 201 us  [per_device(): lax.psum_scatter(grad_acc.astype(jnp.bfloat16), 'dp', scatter_dimension=1...]
    select_n x3, other arithmetic: 3.22 us -> 16.4 us  [per_device(): jnp.where(active_turn, lax.dynamic_update_slice_in_dim(outputs_all, resul...]
    ppermute x0 -> x9, starting transfers between devices: none -> 11.5 us  [the longest x6 9.4 us: block_layer(): earlier_2.append(lax.ppermute(earlier_2[-1], 'tensor', up))]
  transfers between devices with their start and end apart: 10 -> 16, of which waited for: 10 -> 13; matrix products, arithmetic and copies ran while one was open for 3% -> 4% of each run, Pallas kernels for 0% -> 0%
where the time goes in v1:
time: 618 us; the launch traced here: 609 us
  waiting for transfers between devices  340 us (55%)
  local copies, waits for them, and re-layouts  68.7 us (11%)
  other arithmetic  56.7 us (9%)
  matrix products  52 us (8%)
  blocking collectives  30.6 us (5%)
  starting transfers between devices  28.3 us (5%)
  loops' own time  17.3 us (3%)
  between operations  14.8 us (2%)
    reduce_scatter x1, waiting for transfers between devices, per_device(): lax.psum_scatter(grad_acc.astype(jnp.bfloat16), 'dp', scatter_dimension=1...  201 us
    reduce_scatter x3, waiting for transfers between devices, block_layer(): lax.psum_scatter(jnp.dot(y_norm, out_proj, preferred_element_type=jnp.flo...  62.2 us
    all_to_all x1, waiting for transfers between devices, per_device(): lax.all_to_all(outgoing, 'dp', split_axis=0, concat_axis=0, tiled=True)  44.9 us
    psum x3, blocking collectives, block_layer(): sq_sum = lax.psum(jnp.sum(gated * gated, axis=-1), 'tensor')  30.6 us
    ppermute x6, waiting for transfers between devices, block_layer(): earlier_2.append(lax.ppermute(earlier_2[-1], 'tensor', up))  30.1 us
    another operation x3, loops' own time, block_scan(): lax.scan(advance, (state, prev_segment), scanned)  17.3 us
    select_n x3, other arithmetic, per_device(): jnp.where(active_turn, lax.dynamic_update_slice_in_dim(outputs_all, resul...  16.4 us
  transfers between devices with their start and end apart: 16, of which 13 were waited for; matrix products, arithmetic and copies ran while one was open for 4% of the time, Pallas kernels for 0%

profile of v1, /device:TPU:2, one launch (start us, length us, event | category | flops | bytes accessed | tf_op | source)
XLA Modules:
  0.0 608.6 jit_solution(11130930109815143018)
XLA Ops:
  7.2 1.0 select_reduce_fusion.3
  10.8 4.4 scatter_custom_fusion
  15.2 11.8 %all-to-all-start = ((bf16[32,16,2048]{2,1,0:T(8,128)(2,1)}), bf16[32,16,2048]{2,1,0:T(8,128)(2,1)}, u32[]{:S(2)}, u32[]{:S(2)}) async-start(bf16[32,16,2048]{2,1,0:T(8,128)(2,1)} %bitcast.298), calls=%async_computation | async-start | bytes 4194304 | tf_op jit(solution)/shard_map/all_to_all | solution.py:212
  28.2 2.4 scatter_custom_fusion.2
  32.2 44.9 %all-to-all-done = bf16[32,16,2048]{2,1,0:T(8,128)(2,1)} async-done(((bf16[32,16,2048]{2,1,0:T(8,128)(2,1)}), bf16[32,16,2048]{2,1,0:T(8,128)(2,1)}, u32[]{:S(2)}, u32[]{:S(2)}) %all-to-all-start) | async-done | bytes 2097184 | tf_op jit(solution)/shard_map/all_to_all | solution.py:212
  77.1 6.6 %scatter_custom_fusion.1 = bf16[512,2048]{1,0:T(8,128)(2,1)} fusion(s32[512]{0:T(512)S(1)} %bitcast.318, bf16[512,2048]{1,0:T(8,128)(2,1)} %bitcast.30, bf16[]{:T(256)} %constant.141.clone.1), kind=kCustom, calls=%fused_computation.230 | custom fusion | bytes 2097664 | tf_op jit(solution)/shard_map/scatter | solution.py:217
  83.7 1.6 multiply_reduce_fusion.2
  85.4 1.7 compare_select_fusion.2
  87.9 2.2 multiply_convert_fusion.20
  91.9 1.0 broadcast.416.clone2
  92.9 34.9 %while.45 = (s32[]{:T(128)}, f32[8,64,128]{2,1,0:T(8,128)S(1)}, s32[]{:T(128)}, f32[4,64,8,64]{3,2,1,0:T(8,128)}, s32[4,64]{1,0:T(4,128)S(1)}, /*index=5*/f32[4,...) while((s32[]{:T(128)}, f32[8,64,128]{2,1,0:T(8,128)S(1)}, ...), condition=%wide.region_17.18_spmd.clone, body=%wide.region_15.17_spmd.clone.sunk | while | flops 22689996 | bytes 2389582 | solution.py:76
  127.8 1.5 reshape.687
  129.3 2.9 multiply_reduce_fusion.5
  132.2 8.6 %psum.21 = f32[256]{0:T(256)S(1)} all-reduce(f32[256]{0:T(256)S(1)} %get-tuple-element.397), channel_id=1, replica_groups=mesh['dp'=32,'section'=2,'tensor'=4] {'tensor'}, use_global_device_ids=true, to_apply=%region_19.20 | all-reduce | flops 256 | bytes 2048 | tf_op jit(solution)/shard_map/psum | solution.py:124
  140.9 3.4 convolution_convert_fusion.2
  144.3 2.8 fusion.140
  147.1 18.5 %reduce-scatter.5.cloned.1.call-done = bf16[64,2048]{1,0:T(8,128)(2,1)} async-done(((bf16[256,2048]{1,0:T(8,128)(2,1)}), bf16[64,2048]{1,0:T(8,128)(2,1)}) %reduce-scatter.5.cloned.1.call-update) | async-done | bytes 262160 | tf_op jit(solution)/shard_map/reduce_scatter | solution.py:129
  165.6 1.2 add_convert_fusion.3
  166.8 1.9 collective-permute-start
  169.4 4.9 collective-permute-done
  174.3 1.1 collective-permute-start.1
  175.4 6.2 %collective-permute-done.1 = bf16[64,2048]{1,0:T(8,128)(2,1)S(1)} collective-permute-done((bf16[64,2048]{1,0:T(8,128)(2,1)S(1)}, bf16[64,2048]{1,0:T(8,128)(2,1)S(1)}, u32[]{:S(2)}, u32[]{:S(2)}) %collective-permute-start.1) | collective-permute-done | bytes 262176 | tf_op jit(solution)/shard_map/ppermute | solution.py:142
  181.6 1.6 broadcast.410
  183.2 4.7 select_dynamic-update-slice_fusion.1
  187.9 2.4 collective-permute-start.3
  191.8 3.0 fusion.179
  196.9 1.0 copy-done.31
  199.0 1.1 reshape_reshape.10
  200.0 1.0 broadcast.416.clone2.1
  201.1 31.3 %while.43 = (s32[]{:T(128)}, f32[8,64,128]{2,1,0:T(8,128)S(1)}, s32[]{:T(128)}, f32[4,64,8,64]{3,2,1,0:T(8,128)}, s32[4,64]{1,0:T(4,128)}, /*index=5*/f32[4,64,8...) while((s32[]{:T(128)}, f32[8,64,128]{2,1,0:T(8,128)S(1)}, ...), condition=%wide.region_24.26_spmd, body=%wide.region_22.25_spmd.sunk | while | flops 22624460 | bytes 2581539 | solution.py:76
  204.9 0.9 constant_dynamic-slice_fusion.12
  212.8 0.9 constant_dynamic-slice_fusion.12
  232.4 2.3 reshape.692
  234.7 3.0 multiply_reduce_fusion.4
  237.7 11.0 %psum.22 = f32[256]{0:T(256)S(1)} all-reduce(f32[256]{0:T(256)S(1)} %get-tuple-element.399), channel_id=1, replica_groups=mesh['dp'=32,'section'=2,'tensor'=4] {'tensor'}, use_global_device_ids=true, to_apply=%region_26.28 | all-reduce | flops 256 | bytes 2048 | tf_op jit(solution)/shard_map/psum | solution.py:124
  248.7 3.4 convolution_convert_fusion.1
  252.2 23.9 %reduce-scatter.7.cloned.1.call-done = bf16[64,2048]{1,0:T(8,128)(2,1)} async-done(((bf16[256,2048]{1,0:T(8,128)(2,1)}), bf16[64,2048]{1,0:T(8,128)(2,1)}) %reduce-scatter.7.cloned.1.call-update) | async-done | bytes 262160 | tf_op jit(solution)/shard_map/reduce_scatter | solution.py:129
  276.1 1.2 add_convert_fusion.2
  277.3 2.0 collective-permute-start.4
  280.0 4.9 collective-permute-done.4
  284.8 1.1 collective-permute-start.5
  286.0 6.3 %collective-permute-done.5 = bf16[64,2048]{1,0:T(8,128)(2,1)} collective-permute-done((bf16[64,2048]{1,0:T(8,128)(2,1)S(1)}, bf16[64,2048]{1,0:T(8,128)(2,1)}, u32[]{:S(2)}, u32[]{:S(2)}) %collective-permute-start.5) | collective-permute-done | bytes 262176 | tf_op jit(solution)/shard_map/ppermute | solution.py:142
  292.3 5.9 select_dynamic-update-slice_fusion
  298.2 2.5 collective-permute-start.7
  300.8 1.3 collective-permute-done.7
  302.1 3.0 fusion.177
  307.3 1.0 copy-done.32
  309.3 1.1 reshape_reshape.11
  310.3 1.1 broadcast.416.clone
  311.4 24.7 %while.44 = (s32[]{:T(128)}, f32[8,64,128]{2,1,0:T(8,128)S(1)}, s32[]{:T(128)}, f32[4,64,8,64]{3,2,1,0:T(8,128)}, s32[4,64]{1,0:T(4,128)S(1)}, /*index=5*/f32[4,...) while((s32[]{:T(128)}, f32[8,64,128]{2,1,0:T(8,128)S(1)}, ...), condition=%wide.region_31.33_spmd, body=%wide.region_29.32_spmd.sunk | while | flops 22624460 | bytes 2590267 | solution.py:76
  336.1 1.5 reshape.697
  337.6 2.8 multiply_reduce_fusion.3
  340.5 11.0 %psum.23 = f32[256]{0:T(256)S(1)} all-reduce(f32[256]{0:T(256)S(1)} %get-tuple-element.401), channel_id=1, replica_groups=mesh['dp'=32,'section'=2,'tensor'=4] {'tensor'}, use_global_device_ids=true, to_apply=%region_33.35 | all-reduce | flops 256 | bytes 2048 | tf_op jit(solution)/shard_map/psum | solution.py:124
  351.5 3.4 convolution_convert_fusion
  356.8 2.4 add_convert_fusion
  359.3 19.7 %reduce-scatter.9.cloned.1.call-done = bf16[64,2048]{1,0:T(8,128)(2,1)} async-done(((bf16[256,2048]{1,0:T(8,128)(2,1)}), bf16[64,2048]{1,0:T(8,128)(2,1)}) %reduce-scatter.9.cloned.1.call-update) | async-done | bytes 262160 | tf_op jit(solution)/shard_map/reduce_scatter | solution.py:129
  379.0 1.2 add_convert_fusion.1
  380.1 1.9 collective-permute-start.8
  382.8 4.9 collective-permute-done.8
  387.6 1.3 collective-permute-start.9
  389.0 3.2 copy.198
  392.1 3.0 collective-permute-done.9
  395.2 5.7 fusion.104
  400.9 200.9 %reduce-scatter.11.cloned.1.call-done = bf16[512,64]{0,1:T(8,128)(2,1)} async-done(((bf16[512,2048]{0,1:T(8,128)(2,1)}), bf16[512,64]{0,1:T(8,128)(2,1)}) %reduce-scatter.11.cloned.1.call-update) | async-done | bytes 65552 | tf_op jit(solution)/shard_map/reduce_scatter | solution.py:265
  (436 shorter events, 91.4 us)
Async XLA Ops:
  7.2 347.8 %copy-start = (bf16[1,512,2048]{2,1,0:T(8,128)(2,1)S(1)}, bf16[1,512,2048]{2,1,0:T(8,128)(2,1)}, u32[]{:S(2)}) copy-start(bf16[1,512,2048]{2,1,0:T(8,128)(2,1)} %param.25) | copy-start | bytes 6291460
  15.2 11.9 %copy-start.29 = (f32[1,8]{1,0:T(1,128)S(1)}, f32[1,8]{1,0:T(1,128)}, u32[]{:S(2)}) copy-start(f32[1,8]{1,0:T(1,128)} %param.33) | copy-start | bytes 100
  15.2 12.6 %copy-start.21 = (s32[128]{0:T(128)S(1)}, s32[128]{0:T(128)}, u32[]{:S(2)}) copy-start(s32[128]{0:T(128)} %param.24) | copy-start | bytes 1540
  15.2 12.6 %copy-start.20 = (s32[128]{0:T(128)S(1)}, s32[128]{0:T(128)}, u32[]{:S(2)}) copy-start(s32[128]{0:T(128)} %param.23) | copy-start | bytes 1540
  15.2 17.0 %copy-start.42 = (f32[1,8]{1,0:T(1,128)S(1)}, f32[1,8]{1,0:T(1,128)}, u32[]{:S(2)}) copy-start(f32[1,8]{1,0:T(1,128)} %param.32) | copy-start | bytes 100
  15.2 61.9 %all-to-all-start = ((bf16[32,16,2048]{2,1,0:T(8,128)(2,1)}), bf16[32,16,2048]{2,1,0:T(8,128)(2,1)}, u32[]{:S(2)}, u32[]{:S(2)}) async-start(bf16[32,16,2048]{2,1,0:T(8,128)(2,1)} %bitcast.298), calls=%async_computation | async-start | bytes 4194304 | tf_op jit(solution)/shard_map/all_to_all | solution.py:212
  27.0 58.4 %copy-start.35 = (bf16[1,2048,8]{1,2,0:T(8,128)(2,1)S(1)}, bf16[1,2048,8]{1,2,0:T(8,128)(2,1)}, u32[]{:S(2)}) copy-start(bf16[1,2048,8]{1,2,0:T(8,128)(2,1)} %param.30) | copy-start | bytes 98308
  27.0 58.4 %copy-start.38 = (f32[1,2048]{1,0:T(1,128)S(1)}, f32[1,2048]{1,0:T(1,128)}, u32[]{:S(2)}) copy-start(f32[1,2048]{1,0:T(1,128)} %param.26) | copy-start | bytes 24580
  27.0 58.4 %copy-start.43 = (f32[1,8]{1,0:T(1,128)S(1)}, f32[1,8]{1,0:T(1,128)}, u32[]{:S(2)}) copy-start(f32[1,8]{1,0:T(1,128)} %param.31) | copy-start | bytes 100
  27.0 138.6 %reduce-scatter.5.cloned.1.call-start = ((), (), s32[]{:S(2)}) async-start(), calls=%async_computation.5 | async-start | bytes 1310720 | tf_op jit(solution)/shard_map/reduce_scatter | solution.py:129
  85.3 5.4 copy-start.27
  87.9 2.9 copy-start.1
  87.9 2.9 copy-start.30
  92.9 4.5 copy-start.18
  98.2 2.7 copy-start.19
  101.6 4.5 copy-start.18
  106.9 2.7 copy-start.19
  110.4 4.5 copy-start.18
  115.7 2.7 copy-start.19
  119.1 4.5 copy-start.18
  124.4 2.7 copy-start.19
  129.3 11.6 %copy-start.8 = (f32[1,512]{1,0:T(1,128)S(1)}, f32[1,512]{1,0:T(1,128)}, u32[]{:S(2)}) copy-start(f32[1,512]{1,0:T(1,128)} %param.34) | copy-start | bytes 6148
  132.2 12.1 %copy-start.4 = (f32[256,512]{1,0:T(8,128)}, f32[256,512]{1,0:T(8,128)S(1)}, u32[]{:S(2)}) copy-start(f32[256,512]{1,0:T(8,128)S(1)} %get-tuple-element.398) | copy-start | bytes 1572868
  140.9 3.4 copy-start.12
  144.3 131.8 %reduce-scatter.7.cloned.1.call-start = ((), (), s32[]{:S(2)}) async-start(), calls=%async_computation.6 | async-start | bytes 1310720 | tf_op jit(solution)/shard_map/reduce_scatter | solution.py:129
  166.8 7.5 %collective-permute-start = (bf16[64,2048]{1,0:T(8,128)(2,1)S(1)}, bf16[64,2048]{1,0:T(8,128)(2,1)S(1)}, u32[]{:S(2)}, u32[]{:S(2)}) collective-permute-start(bf16[64,2048]{1,0:T(8,128)(2,1)S(1)} %add_convert_fusion.3), channel_id=1, source_target_pairs={{0,1},{1,2},{2,3},{3,0},{4,5},{5,6},{6,7},{7,4},{8,9},{9,10},{10,1... | collective-permute-start | bytes 786440 | tf_op jit(solution)/shard_map/ppermute | solution.py:142
  168.7 6.7 %collective-permute-start.2 = (bf16[64,2048]{1,0:T(8,128)(2,1)S(1)}, bf16[64,2048]{1,0:T(8,128)(2,1)S(1)}, u32[]{:S(2)}, u32[]{:S(2)}) collective-permute-start(bf16[64,2048]{1,0:T(8,128)(2,1)S(1)} %add_convert_fusion.3), channel_id=1, source_target_pairs={{0,3},{1,0},{2,1},{3,2},{4,7},{5,4},{6,5},{7,6},{8,11},{9,8},{10,9... | collective-permute-start | bytes 786440 | tf_op jit(solution)/shard_map/ppermute | solution.py:144
  174.3 7.3 %collective-permute-start.1 = (bf16[64,2048]{1,0:T(8,128)(2,1)S(1)}, bf16[64,2048]{1,0:T(8,128)(2,1)S(1)}, u32[]{:S(2)}, u32[]{:S(2)}) collective-permute-start(bf16[64,2048]{1,0:T(8,128)(2,1)S(1)} %collective-permute-done), channel_id=1, source_target_pairs={{0,1},{1,2},{2,3},{3,0},{4,5},{5,6},{6,7},{7,4},{8,9},{9,10},{10,1... | collective-permute-start | bytes 786440 | tf_op jit(solution)/shard_map/ppermute | solution.py:142
  183.2 7.1 %copy-start.23 = (s32[256]{0:T(256)S(1)}, s32[256]{0:T(256)}, u32[]{:S(2)}) copy-start(s32[256]{0:T(256)} %get-tuple-element.393) | copy-start | bytes 3076
  187.9 3.9 collective-permute-start.3
  191.0 4.1 copy-start.36
  191.0 4.1 copy-start.39
  191.0 4.1 copy-start.44
  194.8 2.2 copy-start.3
  195.1 1.8 copy-start.28
  198.8 2.3 copy-start.10
  237.7 14.4 %copy-start.6 = (f32[256,512]{1,0:T(8,128)}, f32[256,512]{1,0:T(8,128)S(1)}, u32[]{:S(2)}) copy-start(f32[256,512]{1,0:T(8,128)S(1)} %get-tuple-element.400) | copy-start | bytes 1572868
  248.7 3.4 copy-start.14
  252.1 126.8 %reduce-scatter.9.cloned.1.call-start = ((), (), s32[]{:S(2)}) async-start(), calls=%async_computation.7 | async-start | bytes 1310720 | tf_op jit(solution)/shard_map/reduce_scatter | solution.py:129
  277.3 7.6 %collective-permute-start.4 = (bf16[64,2048]{1,0:T(8,128)(2,1)S(1)}, bf16[64,2048]{1,0:T(8,128)(2,1)S(1)}, u32[]{:S(2)}, u32[]{:S(2)}) collective-permute-start(bf16[64,2048]{1,0:T(8,128)(2,1)S(1)} %add_convert_fusion.2), channel_id=1, source_target_pairs={{0,1},{1,2},{2,3},{3,0},{4,5},{5,6},{6,7},{7,4},{8,9},{9,10},{10,1... | collective-permute-start | bytes 786440 | tf_op jit(solution)/shard_map/ppermute | solution.py:142
  279.3 6.7 %collective-permute-start.6 = (bf16[64,2048]{1,0:T(8,128)(2,1)S(1)}, bf16[64,2048]{1,0:T(8,128)(2,1)S(1)}, u32[]{:S(2)}, u32[]{:S(2)}) collective-permute-start(bf16[64,2048]{1,0:T(8,128)(2,1)S(1)} %add_convert_fusion.2), channel_id=1, source_target_pairs={{0,3},{1,0},{2,1},{3,2},{4,7},{5,4},{6,5},{7,6},{8,11},{9,8},{10,9... | collective-permute-start | bytes 786440 | tf_op jit(solution)/shard_map/ppermute | solution.py:144
  284.8 7.4 %collective-permute-start.5 = (bf16[64,2048]{1,0:T(8,128)(2,1)S(1)}, bf16[64,2048]{1,0:T(8,128)(2,1)}, u32[]{:S(2)}, u32[]{:S(2)}) collective-permute-start(bf16[64,2048]{1,0:T(8,128)(2,1)S(1)} %collective-permute-done.4), channel_id=1, source_target_pairs={{0,1},{1,2},{2,3},{3,0},{4,5},{5,6},{6,7},{7,4},{8,9},{9,10},{10,1... | collective-permute-start | bytes 786440 | tf_op jit(solution)/shard_map/ppermute | solution.py:142
  292.3 8.4 %copy-start.22 = (s32[256]{0:T(256)S(1)}, s32[256]{0:T(256)}, u32[]{:S(2)}) copy-start(s32[256]{0:T(256)} %get-tuple-element.392) | copy-start | bytes 3076
  298.2 3.9 collective-permute-start.7
  300.8 4.6 copy-start.37
  300.8 4.6 copy-start.40
  300.8 4.6 copy-start.45
  305.1 2.2 copy-start.2
  305.1 1.6 copy-start.34
  305.4 1.8 copy-start.25
  309.1 2.3 copy-start.9
  311.4 26.2 %copy-start.24 = (f32[512]{0:T(512)S(1)}, f32[512]{0:T(512)}, u32[]{:S(2)}) copy-start(f32[512]{0:T(512)} %mul.552) | copy-start | bytes 6148
  311.4 26.2 %copy-start.26 = (f32[256]{0:T(256)S(1)}, f32[256]{0:T(256)}, u32[]{:S(2)}) copy-start(f32[256]{0:T(256)} %copy-done.25) | copy-start | bytes 3076
  311.4 26.2 %copy-start.41 = (f32[1,2048]{1,0:T(1,128)S(1)}, f32[1,2048]{1,0:T(1,128)}, u32[]{:S(2)}) copy-start(f32[1,2048]{1,0:T(1,128)} %param.26) | copy-start | bytes 24580
  311.4 2.4 copy-start.16
  317.6 2.4 copy-start.16
  323.8 2.4 copy-start.16
  329.9 2.4 copy-start.16
  351.5 3.5 copy-start.5
  351.5 3.5 copy-start.13
  354.9 246.9 %reduce-scatter.11.cloned.1.call-start = ((), (), s32[]{:S(2)}) async-start(), calls=%async_computation.8 | async-start | bytes 2162688 | tf_op jit(solution)/shard_map/reduce_scatter | solution.py:265
  380.1 7.5 %collective-permute-start.8 = (bf16[64,2048]{1,0:T(8,128)(2,1)S(1)}, bf16[64,2048]{1,0:T(8,128)(2,1)S(1)}, u32[]{:S(2)}, u32[]{:S(2)}) collective-permute-start(bf16[64,2048]{1,0:T(8,128)(2,1)S(1)} %add_convert_fusion.1), channel_id=1, source_target_pairs={{0,1},{1,2},{2,3},{3,0},{4,5},{5,6},{6,7},{7,4},{8,9},{9,10},{10,1... | collective-permute-start | bytes 786440 | tf_op jit(solution)/shard_map/ppermute | solution.py:142
  382.0 10.1 %collective-permute-start.10 = (bf16[64,2048]{1,0:T(8,128)(2,1)S(1)}, bf16[64,2048]{1,0:T(8,128)(2,1)S(1)}, u32[]{:S(2)}, u32[]{:S(2)}) collective-permute-start(bf16[64,2048]{1,0:T(8,128)(2,1)S(1)} %add_convert_fusion.1), channel_id=1, source_target_pairs={{0,3},{1,0},{2,1},{3,2},{4,7},{5,4},{6,5},{7,6},{8,11},{9,8},{10,9... | collective-permute-start | bytes 786440 | tf_op jit(solution)/shard_map/ppermute | solution.py:144
  387.6 7.5 %collective-permute-start.9 = (bf16[64,2048]{1,0:T(8,128)(2,1)S(1)}, bf16[64,2048]{1,0:T(8,128)(2,1)S(1)}, u32[]{:S(2)}, u32[]{:S(2)}) collective-permute-start(bf16[64,2048]{1,0:T(8,128)(2,1)S(1)} %collective-permute-done.8), channel_id=1, source_target_pairs={{0,1},{1,2},{2,3},{3,0},{4,5},{5,6},{6,7},{7,4},{8,9},{9,10},{10,1... | collective-permute-start | bytes 786440 | tf_op jit(solution)/shard_map/ppermute | solution.py:142
  (10 other events, 13.4 us)
Sparse Core Ops, SparseCore 0:
  144.4 21.2 reduce-scatter.4
  252.2 23.8 reduce-scatter.6
  355.0 23.9 reduce-scatter.8
  383.7 218.0 reduce-scatter.10
